TPU v7x, 32 devices: a whole 2x2x4 slice. The times are simulated.
32 devices in a mesh: gx: 16 (over z, x, core), gy: 2 (over y).
Axes of the slice: x: 2, y: 2, z: 4, core: 2. Of those that a mesh axis runs over, the one named last changes fastest.
Arguments:
- vectors: bfloat16 [64, 16, 128, 128], P('gx', 'gy'), may hold values from -6 to 6
- hamiltonian: bfloat16 [64, 16, 9, 128, 128], P('gx', 'gy'), may hold values from -0.125 to 0.125
- neighbours: int32 [64, 16, 9], P('gx', 'gy'), may hold values from 0 to 8, each once within a row
Outputs:
- filtered: float32 [64, 16, 128, 128], P('gx', 'gy')
Inputs may be any that keep to these rules, and one draw needn't show every extreme that they name: `neighbours`: each cell's list names every offset code 0 to 8 exactly once, in any order.
All inputs are finite; a program needn't handle non-finite values.
Results may differ from a plain program's by a relative error of at most 0.0034.
Values may be sent and summed in bfloat16 or wider, within the bound.
A program may use at most 128 MiB of HBM per device.

v0:
```python
import functools

import jax
import jax.numpy as jnp
from jax import lax
from jax.experimental import pallas as pl
from jax.experimental.pallas import tpu as pltpu
from jax.sharding import PartitionSpec as P

STEPS = 4
NBR = 9
MESH = pl.DeviceIdType.MESH


def filter_kernel(nx, ny, nb_ref, v_hbm, h_hbm, out_hbm, vbuf, hbuf, ybuf, inv,
                  row_send, row_recv, col_send, col_recv, v_sem, h_sem, out_sem):
    rows, cols = v_hbm.shape[0], v_hbm.shape[1]
    gx, gy = lax.axis_index("gx"), lax.axis_index("gy")
    up = (lax.rem(gx + nx - 1, nx), gy)
    down = (lax.rem(gx + 1, nx), gy)
    left = (gx, lax.rem(gy + ny - 1, ny))
    right = (gx, lax.rem(gy + 1, ny))

    parity = lax.rem(gx, 2)
    across = jnp.where(parity == 0, up[0], down[0])
    diagonals = ((across, left[1]), (across, right[1]))

    mirrored = lax.rem(gy, 2) == 1

    def at(p, length):
        return jnp.where(mirrored, length - 1 - p, p)

    near_send = jnp.where(mirrored, 1, 0)
    barrier = pltpu.get_barrier_semaphore()
    for neighbour in (up, down, left, right) + diagonals:
        pl.semaphore_signal(barrier, inc=1, device_id=neighbour, device_id_type=MESH)

    v_copy = pltpu.make_async_copy(v_hbm, vbuf.at[0, pl.ds(1, rows), pl.ds(1, cols)], v_sem)
    v_copy.start()
    h_copies = []
    for r in range(rows):
        h_copies.append(pltpu.make_async_copy(h_hbm.at[r], hbuf.at[r], h_sem.at[r]))
        h_copies[-1].start()

    def row_copy(slot, way, c, source=None):
        src_row, dst_row, device = ((1, rows + 1, up), (rows, 0, down))[way]
        src = vbuf.at[slot, src_row, c] if source is None else source
        return pltpu.make_async_remote_copy(
            src_ref=src, dst_ref=vbuf.at[slot, dst_row, c],
            send_sem=row_send.at[slot, way, c], recv_sem=row_recv.at[slot, way, c],
            device_id=device, device_id_type=MESH)

    def ends(way):
        return (jnp.where(way == 0, 1, cols), jnp.where(way == 0, cols + 1, 0),
                jnp.where(way == 0, left[1], right[1]))

    def diagonal_copy(slot, way, side_way, source=None):
        src_row, dst_row = ((1, rows + 1), (rows, 0))[way]
        src_col, dst_col, place = ends(side_way)
        src = vbuf.at[slot, src_row, src_col]
        if source is not None:
            src = source.at[src_row - 1, src_col - 1]
        return pltpu.make_async_remote_copy(
            src_ref=src, dst_ref=vbuf.at[slot, dst_row, dst_col],
            send_sem=row_send.at[slot, way, dst_col], recv_sem=row_recv.at[slot, way, dst_col],
            device_id=(across, place), device_id_type=MESH)

    def send_corner(slot, side, source=None):
        for way in range(2):
            @pl.when(parity == way)
            def _():
                diagonal_copy(slot, way, send_way(side), source).start()

    def send_way(side):
        return near_send if side == 0 else 1 - near_send

    def col_copy(slot, way, piece, source=None):
        src_col, dst_col, place = ends(way)
        first, count = ((1, 1), (rows, 1), (2, rows - 2))[piece]
        src = vbuf.at[slot, pl.ds(first, count), src_col]
        if source is not None:
            src = source.at[pl.ds(first - 1, count), src_col - 1]
        return pltpu.make_async_remote_copy(
            src_ref=src, dst_ref=vbuf.at[slot, pl.ds(first, count), dst_col],
            send_sem=col_send.at[slot, way, piece], recv_sem=col_recv.at[slot, way, piece],
            device_id=(gx, place), device_id_type=MESH)

    half = (cols + 1) // 2
    halves = (tuple(range(half)), tuple(range(cols - 1, half - 1, -1)))

    pl.semaphore_wait(barrier, 6)

    def pass_corner(slot, side):
        place = at(0 if side == 0 else cols + 1, cols + 2)
        for way in range(2):
            @pl.when(parity != way)
            def _():
                row_copy(slot, way, place).start()

    for side in range(2):
        send_corner(0, side, v_hbm)
        for number, p in enumerate(halves[side]):
            j = at(p, cols)
            row_copy(0, 0, j + 1, v_hbm.at[0, j]).start()
            row_copy(0, 1, j + 1, v_hbm.at[rows - 1, j]).start()
            if number == 0:
                for piece in range(3):
                    col_copy(0, send_way(side), piece, v_hbm).start()

    def invert(cell, carry):
        r, c = cell // cols, cell % cols
        packed = jnp.int32(0)
        for k in range(NBR):
            code = nb_ref[r, c, k]
            packed = packed + jnp.where(code == NBR - 1, 0, jnp.int32(k) << ((code & 7) * 4))
        total = jnp.int32(0)
        for o in range(NBR - 1):
            entry = jnp.minimum(lax.shift_right_logical(packed, jnp.int32(4 * o)) & 15, NBR - 1)
            inv[cell * NBR + o] = entry
            total = total + entry
        inv[cell * NBR + NBR - 1] = jnp.clip(NBR * (NBR - 1) // 2 - total, 0, NBR - 1)
        return carry

    lax.fori_loop(0, rows * cols, invert, 0)

    v_copy.wait()

    def start_values(r, carry):
        for c in range(cols):
            ybuf[0, r, c] = vbuf[0, r + 1, c + 1].astype(jnp.float32)
            ybuf[1, r, c] = jnp.zeros(ybuf.shape[3:], jnp.float32)
        return carry

    lax.fori_loop(0, rows, start_values, 0)
    for copy in h_copies:
        copy.wait()

    def out_copy(r, c):
        return pltpu.make_async_copy(ybuf.at[0, r, c], out_hbm.at[r, c], out_sem.at[r, c])

    def step(k, last):
        factor = jnp.where(k == 0, 1.0, 2.0).astype(jnp.float32)
        kept = lax.rem(k + 1, 2)

        def cells(places):
            for r, c in places:
                base = (r * cols + c) * NBR
                lhs = jnp.concatenate([hbuf[r, c, inv[base + o]] for o in range(NBR)], axis=1)
                rhs = jnp.concatenate(
                    [vbuf[k, r + o // 3, c + o % 3] for o in range(NBR)], axis=0)
                acc = jnp.dot(lhs, rhs, preferred_element_type=jnp.float32)
                new = factor * acc - ybuf[kept, r, c]
                ybuf[kept, r, c] = new
                if not last:
                    vbuf[k + 1, r + 1, c + 1] = new.astype(jnp.bfloat16)
            if last:
                for r, c in places:
                    out_copy(r, c).start()

        waited = set()

        def rim(p, side=None):
            j = at(p, cols)
            for q in (p, p + 1, p + 2):
                if q not in waited:
                    waited.add(q)
                    for way in range(2):
                        row_copy(k, way, at(q, cols + 2)).wait_recv()
            cells([(0, j), (rows - 1, j)])
            if not last:
                if side is not None:
                    send_corner(k + 1, side)
                    for piece in range(2):
                        col_copy(k + 1, send_way(side), piece).start()
                for way in range(2):
                    row_copy(k + 1, way, j + 1).start()

        for side in range(2):
            edge = halves[side][0]
            for piece in range(2):
                col_copy(k, 1 - send_way(side), piece).wait_recv()
            pass_corner(k, side)
            col_copy(k, 1 - send_way(side), 2).wait_recv()
            cells([(r, at(edge, cols)) for r in range(1, rows - 1)])
            if not last:
                col_copy(k + 1, send_way(side), 2).start()
            rim(edge, side)
            for p in halves[side][1:]:
                rim(p)

        for side in range(2):
            for p in halves[side][1:]:
                cells([(r, at(p, cols)) for r in range(1, rows - 1)])

    def looped(k, carry):
        step(k, False)
        return carry

    lax.fori_loop(0, STEPS - 1, looped, 0)
    step(STEPS - 1, True)

    def drain(k, carry):
        for way in range(2):
            for c in range(cols + 2):
                row_copy(k, way, c).wait_send()
            for piece in range(3):
                col_copy(k, way, piece).wait_send()
        return carry

    lax.fori_loop(0, STEPS, drain, 0)
    for r in range(rows):
        for c in range(cols):
            out_copy(r, c).wait()


def on_device(nx, ny, vectors, hamiltonian, neighbours):
    rows, cols, height, width = vectors.shape
    return pl.pallas_call(
        functools.partial(filter_kernel, nx, ny),
        out_shape=jax.ShapeDtypeStruct(vectors.shape, jnp.float32),
        in_specs=[
            pl.BlockSpec(memory_space=pltpu.SMEM),
            pl.BlockSpec(memory_space=pl.ANY),
            pl.BlockSpec(memory_space=pl.ANY),
        ],
        out_specs=pl.BlockSpec(memory_space=pl.ANY),
        scratch_shapes=[
            pltpu.VMEM((STEPS, rows + 2, cols + 2, height, width), jnp.bfloat16),
            pltpu.VMEM(hamiltonian.shape, jnp.bfloat16),
            pltpu.VMEM((2,) + vectors.shape, jnp.float32),
            pltpu.SMEM((rows * cols * NBR,), jnp.int32),
            pltpu.SemaphoreType.DMA((STEPS, 2, cols + 2)),
            pltpu.SemaphoreType.DMA((STEPS, 2, cols + 2)),
            pltpu.SemaphoreType.DMA((STEPS, 2, 3)),
            pltpu.SemaphoreType.DMA((STEPS, 2, 3)),
            pltpu.SemaphoreType.DMA,
            pltpu.SemaphoreType.DMA((rows,)),
            pltpu.SemaphoreType.DMA((rows, cols)),
        ],
        compiler_params=pltpu.CompilerParams(
            collective_id=0, has_side_effects=True, vmem_limit_bytes=60 * 1024 * 1024),
    )(neighbours, vectors, hamiltonian)


def solution(mesh):
    placed = (P("gx", "gy", None, None), P("gx", "gy", None, None, None), P("gx", "gy", None))
    return jax.shard_map(
        functools.partial(on_device, mesh.shape["gx"], mesh.shape["gy"]),
        mesh=mesh, in_specs=placed, out_specs=P("gx", "gy", None, None), check_vma=False
    )
```

profile of v0, /device:TPU:1, one launch (start us, length us, event | category | flops | bytes accessed | tf_op | source)
XLA Modules:
  0.0 46.9 jit_solution(11064399157486768195)
XLA Ops:
  0.0 43.7 %shard_map.37 = f32[4,8,128,128]{3,2,1,0:T(8,128)} custom-call(s32[4,8,9]{2,1,0:T(8,128)} %nb_ref.1, bf16[4,8,128,128]{3,2,1,0:T(8,128)(2,1)} %v_hbm.1, bf16[4,8,9,128,128]{4,3,2,1,0:T(8,128)(2,1)} %h_hbm.1), custom_call_target="tpu_custom_call" | custom-call | tf_op jit(solution)/shard_map/pallas_call | solution.py:218
  43.7 3.1 %copy.5 = f32[4,8,128,128]{3,2,1,0:T(8,128)} copy(f32[4,8,128,128]{3,2,1,0:T(8,128)} %shard_map.37) | data formatting | bytes 4194304
where the time goes:
time: 47.1 us; the launch traced here: 46.9 us
  Pallas kernels  43.7 us (93%)
  local copies, waits for them, and re-layouts  3.14 us (7%)
    pallas_call x1, Pallas kernels, on_device(): pl.pallas_call(functools.partial(filter_kernel, nx, ny), out_shape=jax.Sh...  43.7 us
    unnamed x1, local copies, waits for them, and re-layouts  3.14 us

commit v1 on v0

v1 whole, which is shorter than its diff:
```python
import functools

import jax
import jax.numpy as jnp
from jax import lax
from jax.experimental import pallas as pl
from jax.experimental.pallas import tpu as pltpu
from jax.sharding import PartitionSpec as P

STEPS = 4
NBR = 9
MESH = pl.DeviceIdType.MESH
OFF, ON = 0, 1


def filter_kernel(nx, ny, nb_ref, v_hbm, h_hbm, out_ref, vbuf, hbuf, ybuf, inv,
                  row_send, row_recv, col_send, col_recv, v_sem, h_sem):
    rows, cols = v_hbm.shape[0], v_hbm.shape[1]
    gx, gy = lax.axis_index("gx"), lax.axis_index("gy")
    up = lax.rem(gx + nx - 1, nx)
    down = lax.rem(gx + 1, nx)
    left = lax.rem(gy + ny - 1, ny)
    right = lax.rem(gy + 1, ny)

    even = lax.rem(gx, 2) == 0
    peer = (jnp.where(even, up, down), jnp.where(even, down, up))
    own_row = (jnp.where(even, 1, rows), jnp.where(even, rows, 1))
    halo_row = (jnp.where(even, 0, rows + 1), jnp.where(even, rows + 1, 0))
    far = lax.rem(jnp.where(even, up, gx), 4) == 3
    near = jnp.logical_not(far)
    mirrored = lax.rem(gy, 2) == 1

    def at(p, length):
        return jnp.where(mirrored, length - 1 - p, p)

    def leftward(side):
        return mirrored if side == 1 else jnp.logical_not(mirrored)

    def ends(side):
        to_left = leftward(side)
        return (jnp.where(to_left, 1, cols), jnp.where(to_left, cols + 1, 0),
                jnp.where(to_left, left, right))

    beside = (left,) if ny == 2 else (left, right)
    barrier = pltpu.get_barrier_semaphore()

    def greet(device):
        pl.semaphore_signal(barrier, inc=1, device_id=device, device_id_type=MESH)

    for place in beside:
        greet((gx, place))
    for kind in (OFF, ON):
        greet((peer[kind], gy))

    @pl.when(far)
    def _():
        for place in beside:
            greet((peer[OFF], place))

    v_copy = pltpu.make_async_copy(v_hbm, vbuf.at[0, pl.ds(1, rows), pl.ds(1, cols)], v_sem)
    v_copy.start()
    h_copies = []
    for r in range(rows):
        h_copies.append(pltpu.make_async_copy(h_hbm.at[r], hbuf.at[r], h_sem.at[r]))
        h_copies[-1].start()

    def row_copy(slot, kind, c, source=None):
        src = vbuf.at[slot, own_row[kind], c]
        if source is not None:
            src = source.at[own_row[kind] - 1, c - 1]
        return pltpu.make_async_remote_copy(
            src_ref=src, dst_ref=vbuf.at[slot, rows + 1 - halo_row[kind], c],
            send_sem=row_send.at[slot, kind, c], recv_sem=row_recv.at[slot, kind, c],
            device_id=(peer[kind], gy), device_id_type=MESH)

    def corner_copy(slot, side, source=None):
        src_col, dst_col, place = ends(side)
        src = vbuf.at[slot, own_row[OFF], src_col]
        if source is not None:
            src = source.at[own_row[OFF] - 1, src_col - 1]
        return pltpu.make_async_remote_copy(
            src_ref=src, dst_ref=vbuf.at[slot, rows + 1 - halo_row[OFF], dst_col],
            send_sem=row_send.at[slot, OFF, dst_col], recv_sem=row_recv.at[slot, OFF, dst_col],
            device_id=(peer[OFF], place), device_id_type=MESH)

    def relay_copy(slot, side):
        src_col, dst_col, place = ends(side)
        return pltpu.make_async_remote_copy(
            src_ref=vbuf.at[slot, halo_row[OFF], src_col], dst_ref=vbuf.at[slot, halo_row[OFF], dst_col],
            send_sem=row_send.at[slot, OFF, dst_col], recv_sem=row_recv.at[slot, OFF, dst_col],
            device_id=(gx, place), device_id_type=MESH)

    def col_copy(slot, side, piece, source=None):
        src_col, dst_col, place = ends(side)
        first, count = ((own_row[ON], 1), (own_row[OFF], 1), (2, rows - 2))[piece]
        src = vbuf.at[slot, pl.ds(first, count), src_col]
        if source is not None:
            src = source.at[pl.ds(first - 1, count), src_col - 1]
        return pltpu.make_async_remote_copy(
            src_ref=src, dst_ref=vbuf.at[slot, pl.ds(first, count), dst_col],
            send_sem=col_send.at[slot, side, piece], recv_sem=col_recv.at[slot, side, piece],
            device_id=(gx, place), device_id_type=MESH)

    half = (cols + 1) // 2
    halves = (tuple(range(half)), tuple(range(cols - 1, half - 1, -1)))

    def corner_place(side):
        return at(0 if side == 0 else cols + 1, cols + 2)

    def end_place(side):
        return at(1 if side == 0 else cols, cols + 2)

    def relay(slot, side):
        @pl.when(near)
        def _():
            row_copy(slot, OFF, end_place(side)).wait_recv()
            relay_copy(slot, side).start()
        col_copy(slot, side, 0).wait_recv()
        row_copy(slot, ON, corner_place(side)).start()

    pl.semaphore_wait(barrier, 2 + len(beside) + jnp.where(far, len(beside), 0))

    for side in range(2):
        @pl.when(far)
        def _():
            corner_copy(0, side, v_hbm).start()
        for number, p in enumerate(halves[side]):
            c = at(p, cols) + 1
            row_copy(0, OFF, c, v_hbm).start()
            if number == 0 and side == 0:
                for piece in range(3):
                    col_copy(0, side, piece, v_hbm).start()
            row_copy(0, ON, c, v_hbm).start()

    def invert(cell, carry):
        r, c = cell // cols, cell % cols
        packed = jnp.int32(0)
        for k in range(NBR):
            code = nb_ref[r, c, k]
            packed = packed + jnp.where(code == NBR - 1, 0, jnp.int32(k) << ((code & 7) * 4))
        total = jnp.int32(0)
        for o in range(NBR - 1):
            entry = jnp.minimum(lax.shift_right_logical(packed, jnp.int32(4 * o)) & 15, NBR - 1)
            inv[cell * NBR + o] = entry
            total = total + entry
        inv[cell * NBR + NBR - 1] = jnp.clip(NBR * (NBR - 1) // 2 - total, 0, NBR - 1)
        return carry

    lax.fori_loop(0, rows * cols, invert, 0)

    v_copy.wait()

    def start_values(r, carry):
        for c in range(cols):
            ybuf[0, r, c] = vbuf[0, r + 1, c + 1].astype(jnp.float32)
            ybuf[1, r, c] = jnp.zeros(ybuf.shape[3:], jnp.float32)
        return carry

    lax.fori_loop(0, rows, start_values, 0)
    for copy in h_copies:
        copy.wait()

    def step(k, first, last):
        factor = 1.0 if first else jnp.float32(2.0)
        kept = lax.rem(k + 1, 2)

        def cells(places):
            for r, c in places:
                base = (r * cols + c) * NBR
                lhs = jnp.concatenate([hbuf[r, c, inv[base + o]] for o in range(NBR)], axis=1)
                rhs = jnp.concatenate(
                    [vbuf[k, r + o // 3, c + o % 3] for o in range(NBR)], axis=0)
                acc = jnp.dot(lhs, rhs, preferred_element_type=jnp.float32)
                new = factor * acc - ybuf[kept, r, c]
                if last:
                    out_ref[r, c] = new
                else:
                    ybuf[kept, r, c] = new
                    vbuf[k + 1, r + 1, c + 1] = new.astype(jnp.bfloat16)

        def inside(side):
            for p in halves[side][1:]:
                cells([(r, at(p, cols)) for r in range(1, rows - 1)])

        waited = set()

        def await_rows(p):
            for q in (p + 1, p + 2, p):
                if q in waited:
                    continue
                waited.add(q)
                place = at(q, cols + 2)
                if q in (1, cols):
                    @pl.when(far)
                    def _():
                        row_copy(k, OFF, place).wait_recv()
                else:
                    row_copy(k, OFF, place).wait_recv()
                row_copy(k, ON, place).wait_recv()

        def process(side):
            edge = halves[side][0]
            for piece in (1, 2):
                col_copy(k, side, piece).wait_recv()
            for p in halves[side]:
                await_rows(p)
                j = at(p, cols)
                cells([(0, j), (rows - 1, j)])
                if not last:
                    row_copy(k + 1, OFF, j + 1).start()
                    if p == edge:
                        @pl.when(far)
                        def _():
                            corner_copy(k + 1, side).start()
                        for piece in range(2):
                            col_copy(k + 1, side, piece).start()
                    row_copy(k + 1, ON, j + 1).start()
                if p == edge:
                    cells([(r, j) for r in range(1, rows - 1)])
                    if not last:
                        col_copy(k + 1, side, 2).start()

        if first:
            inside(0)
            relay(0, 0)
            for piece in range(3):
                col_copy(0, 1, piece, v_hbm).start()
            inside(1)
            relay(0, 1)
            process(0)
            relay(1, 0)
            process(1)
            relay(1, 1)
        elif last:
            inside(0)
            inside(1)
            process(0)
            process(1)
        else:
            process(0)
            inside(0)
            relay(k + 1, 0)
            process(1)
            inside(1)
            relay(k + 1, 1)

    step(0, True, False)

    def looped(k, carry):
        step(k, False, False)
        return carry

    lax.fori_loop(1, STEPS - 1, looped, 0)
    step(STEPS - 1, False, True)

    def drain(k, carry):
        for kind in range(2):
            for c in range(cols + 2):
                row_copy(k, kind, c).wait_send()
            for piece in range(3):
                col_copy(k, kind, piece).wait_send()
        return carry

    lax.fori_loop(0, STEPS, drain, 0)


def on_device(nx, ny, vectors, hamiltonian, neighbours):
    rows, cols, height, width = vectors.shape
    vectors, hamiltonian, neighbours = (
        pltpu.with_memory_space_constraint(x, pltpu.HBM) for x in (vectors, hamiltonian, neighbours))
    return pl.pallas_call(
        functools.partial(filter_kernel, nx, ny),
        out_shape=jax.ShapeDtypeStruct(vectors.shape, jnp.float32),
        in_specs=[
            pl.BlockSpec(memory_space=pltpu.SMEM),
            pl.BlockSpec(memory_space=pltpu.HBM),
            pl.BlockSpec(memory_space=pltpu.HBM),
        ],
        out_specs=pl.BlockSpec(memory_space=pltpu.VMEM),
        scratch_shapes=[
            pltpu.VMEM((STEPS, rows + 2, cols + 2, height, width), jnp.bfloat16),
            pltpu.VMEM(hamiltonian.shape, jnp.bfloat16),
            pltpu.VMEM((2,) + vectors.shape, jnp.float32),
            pltpu.SMEM((rows * cols * NBR,), jnp.int32),
            pltpu.SemaphoreType.DMA((STEPS, 2, cols + 2)),
            pltpu.SemaphoreType.DMA((STEPS, 2, cols + 2)),
            pltpu.SemaphoreType.DMA((STEPS, 2, 3)),
            pltpu.SemaphoreType.DMA((STEPS, 2, 3)),
            pltpu.SemaphoreType.DMA,
            pltpu.SemaphoreType.DMA((rows,)),
        ],
        compiler_params=pltpu.CompilerParams(
            collective_id=0, has_side_effects=True, vmem_limit_bytes=32 * 1024 * 1024),
    )(neighbours, vectors, hamiltonian)


def solution(mesh):
    placed = (P("gx", "gy", None, None), P("gx", "gy", None, None, None), P("gx", "gy", None))
    return jax.shard_map(
        functools.partial(on_device, mesh.shape["gx"], mesh.shape["gy"]),
        mesh=mesh, in_specs=placed, out_specs=P("gx", "gy", None, None), check_vma=False
    )
```

time: 47.1 us -> 42.6 us (0.904)
  Pallas kernels: 43.7 us -> 41.1 us
  local copies, waits for them, and re-layouts: 3.14 us -> 1.32 us
    pallas_call x1, Pallas kernels: 43.7 us -> 41.1 us  [on_device(): pl.pallas_call(functools.partial(filter_kernel, nx, ny), out_shape=jax.Sh...]
    unnamed x1, local copies, waits for them, and re-layouts: 3.14 us -> 1.32 us
where the time goes in v1:
time: 42.6 us; the launch traced here: 42.4 us
  Pallas kernels  41.1 us (96%)
  local copies, waits for them, and re-layouts  1.32 us (3%)
    pallas_call x1, Pallas kernels, on_device(): pl.pallas_call(functools.partial(filter_kernel, nx, ny), out_shape=jax.Sh...  41.1 us
    unnamed x1, local copies, waits for them, and re-layouts  1.32 us

profile of v1, /device:TPU:1, one launch (start us, length us, event | category | flops | bytes accessed | tf_op | source)
XLA Modules:
  0.0 42.4 jit_solution(4239935647406230528)
XLA Ops:
  0.0 41.1 %shard_map.37 = f32[4,8,128,128]{3,2,1,0:T(8,128)S(1)} custom-call(s32[4,8,9]{2,1,0:T(8,128)} %nb_ref.1, bf16[4,8,128,128]{3,2,1,0:T(8,128)(2,1)} %v_hbm.1, bf16[4,8,9,128,128]{4,3,2,1,0:T(8,128)(2,1)} %h_hbm.1), custom_call_target="tpu_custom_call" | custom-call | tf_op jit(solution)/shard_map/pallas_call | solution.py:271
  41.1 1.3 %copy.5 = f32[4,8,128,128]{3,2,1,0:T(8,128)} copy(f32[4,8,128,128]{3,2,1,0:T(8,128)S(1)} %shard_map.37) | data formatting | bytes 4194304

commit v2 on v1

--- a/solution.py
+++ b/solution.py
@@ -26,8 +26,6 @@
     peer = (jnp.where(even, up, down), jnp.where(even, down, up))
     own_row = (jnp.where(even, 1, rows), jnp.where(even, rows, 1))
     halo_row = (jnp.where(even, 0, rows + 1), jnp.where(even, rows + 1, 0))
-    far = lax.rem(jnp.where(even, up, gx), 4) == 3
-    near = jnp.logical_not(far)
     mirrored = lax.rem(gy, 2) == 1
 
     def at(p, length):
@@ -52,10 +50,8 @@
     for kind in (OFF, ON):
         greet((peer[kind], gy))
 
-    @pl.when(far)
-    def _():
-        for place in beside:
-            greet((peer[OFF], place))
+    for place in beside:
+        greet((peer[OFF], place))
 
     v_copy = pltpu.make_async_copy(v_hbm, vbuf.at[0, pl.ds(1, rows), pl.ds(1, cols)], v_sem)
     v_copy.start()
@@ -82,13 +78,6 @@
             src_ref=src, dst_ref=vbuf.at[slot, rows + 1 - halo_row[OFF], dst_col],
             send_sem=row_send.at[slot, OFF, dst_col], recv_sem=row_recv.at[slot, OFF, dst_col],
             device_id=(peer[OFF], place), device_id_type=MESH)
-
-    def relay_copy(slot, side):
-        src_col, dst_col, place = ends(side)
-        return pltpu.make_async_remote_copy(
-            src_ref=vbuf.at[slot, halo_row[OFF], src_col], dst_ref=vbuf.at[slot, halo_row[OFF], dst_col],
-            send_sem=row_send.at[slot, OFF, dst_col], recv_sem=row_recv.at[slot, OFF, dst_col],
-            device_id=(gx, place), device_id_type=MESH)
 
     def col_copy(slot, side, piece, source=None):
         src_col, dst_col, place = ends(side)
@@ -101,36 +90,24 @@
             send_sem=col_send.at[slot, side, piece], recv_sem=col_recv.at[slot, side, piece],
             device_id=(gx, place), device_id_type=MESH)
 
-    half = (cols + 1) // 2
-    halves = (tuple(range(half)), tuple(range(cols - 1, half - 1, -1)))
-
     def corner_place(side):
         return at(0 if side == 0 else cols + 1, cols + 2)
 
-    def end_place(side):
-        return at(1 if side == 0 else cols, cols + 2)
-
-    def relay(slot, side):
-        @pl.when(near)
-        def _():
-            row_copy(slot, OFF, end_place(side)).wait_recv()
-            relay_copy(slot, side).start()
+    def hand_on(slot, side):
         col_copy(slot, side, 0).wait_recv()
         row_copy(slot, ON, corner_place(side)).start()
 
-    pl.semaphore_wait(barrier, 2 + len(beside) + jnp.where(far, len(beside), 0))
-
-    for side in range(2):
-        @pl.when(far)
-        def _():
-            corner_copy(0, side, v_hbm).start()
-        for number, p in enumerate(halves[side]):
-            c = at(p, cols) + 1
-            row_copy(0, OFF, c, v_hbm).start()
-            if number == 0 and side == 0:
-                for piece in range(3):
-                    col_copy(0, side, piece, v_hbm).start()
-            row_copy(0, ON, c, v_hbm).start()
+    pl.semaphore_wait(barrier, 2 + 2 * len(beside))
+
+    for p in range(cols):
+        c = at(p, cols) + 1
+        if p in (0, cols - 1):
+            corner_copy(0, 0 if p == 0 else 1, v_hbm).start()
+        row_copy(0, OFF, c, v_hbm).start()
+        if p in (0, cols - 1):
+            for piece in range(3):
+                col_copy(0, 0 if p == 0 else 1, piece, v_hbm).start()
+        row_copy(0, ON, c, v_hbm).start()
 
     def invert(cell, carry):
         r, c = cell // cols, cell % cols
@@ -178,9 +155,8 @@
                     ybuf[kept, r, c] = new
                     vbuf[k + 1, r + 1, c + 1] = new.astype(jnp.bfloat16)
 
-        def inside(side):
-            for p in halves[side][1:]:
-                cells([(r, at(p, cols)) for r in range(1, rows - 1)])
+        def inside(p):
+            cells([(r, at(p, cols)) for r in range(1, rows - 1)])
 
         waited = set()
 
@@ -190,59 +166,39 @@
                     continue
                 waited.add(q)
                 place = at(q, cols + 2)
-                if q in (1, cols):
-                    @pl.when(far)
-                    def _():
-                        row_copy(k, OFF, place).wait_recv()
-                else:
-                    row_copy(k, OFF, place).wait_recv()
+                row_copy(k, OFF, place).wait_recv()
                 row_copy(k, ON, place).wait_recv()
 
-        def process(side):
-            edge = halves[side][0]
-            for piece in (1, 2):
-                col_copy(k, side, piece).wait_recv()
-            for p in halves[side]:
-                await_rows(p)
-                j = at(p, cols)
-                cells([(0, j), (rows - 1, j)])
-                if not last:
-                    row_copy(k + 1, OFF, j + 1).start()
-                    if p == edge:
-                        @pl.when(far)
-                        def _():
-                            corner_copy(k + 1, side).start()
-                        for piece in range(2):
-                            col_copy(k + 1, side, piece).start()
-                    row_copy(k + 1, ON, j + 1).start()
-                if p == edge:
-                    cells([(r, j) for r in range(1, rows - 1)])
-                    if not last:
-                        col_copy(k + 1, side, 2).start()
-
+        if first or last:
+            for p in range(1, cols - 1):
+                inside(p)
         if first:
-            inside(0)
-            relay(0, 0)
-            for piece in range(3):
-                col_copy(0, 1, piece, v_hbm).start()
-            inside(1)
-            relay(0, 1)
-            process(0)
-            relay(1, 0)
-            process(1)
-            relay(1, 1)
-        elif last:
-            inside(0)
-            inside(1)
-            process(0)
-            process(1)
-        else:
-            process(0)
-            inside(0)
-            relay(k + 1, 0)
-            process(1)
-            inside(1)
-            relay(k + 1, 1)
+            hand_on(0, 0)
+        for p in range(cols):
+            j = at(p, cols)
+            side = {0: 0, cols - 1: 1}.get(p)
+            if p == cols // 2 + 1:
+                hand_on(k, 1)
+            if side is not None:
+                for piece in (1, 2):
+                    col_copy(k, side, piece).wait_recv()
+            if last and p == cols - 1:
+                inside(p)
+            await_rows(p)
+            cells([(0, j), (rows - 1, j)])
+            if not last:
+                row_copy(k + 1, OFF, j + 1).start()
+                if side is not None:
+                    corner_copy(k + 1, side).start()
+                    for piece in range(2):
+                        col_copy(k + 1, side, piece).start()
+                row_copy(k + 1, ON, j + 1).start()
+            if (side is not None or not (first or last)) and not (last and p == cols - 1):
+                inside(p)
+            if side is not None and not last:
+                col_copy(k + 1, side, 2).start()
+        if not last:
+            hand_on(k + 1, 0)
 
     step(0, True, False)
 

time: 42.6 us -> 40 us (0.939)
  Pallas kernels: 41.1 us -> 38.2 us
    pallas_call x1, Pallas kernels: 41.1 us -> 38.2 us  [on_device(): pl.pallas_call(functools.partial(filter_kernel, nx, ny), out_shape=jax.Sh...]
where the time goes in v2:
time: 40 us; the launch traced here: 39.5 us
  Pallas kernels  38.2 us (96%)
  local copies, waits for them, and re-layouts  1.32 us (3%)
    pallas_call x1, Pallas kernels, on_device(): pl.pallas_call(functools.partial(filter_kernel, nx, ny), out_shape=jax.Sh...  38.2 us
    unnamed x1, local copies, waits for them, and re-layouts  1.32 us

profile of v2, /device:TPU:1, one launch (start us, length us, event | category | flops | bytes accessed | tf_op | source)
XLA Modules:
  0.0 39.5 jit_solution(865965565997706108)
XLA Ops:
  0.0 38.2 %shard_map.37 = f32[4,8,128,128]{3,2,1,0:T(8,128)S(1)} custom-call(s32[4,8,9]{2,1,0:T(8,128)} %nb_ref.1, bf16[4,8,128,128]{3,2,1,0:T(8,128)(2,1)} %v_hbm.1, bf16[4,8,9,128,128]{4,3,2,1,0:T(8,128)(2,1)} %h_hbm.1), custom_call_target="tpu_custom_call" | custom-call | tf_op jit(solution)/shard_map/pallas_call | solution.py:227
  38.2 1.3 %copy.5 = f32[4,8,128,128]{3,2,1,0:T(8,128)} copy(f32[4,8,128,128]{3,2,1,0:T(8,128)S(1)} %shard_map.37) | data formatting | bytes 4194304

commit v3 on v2

--- a/solution.py
+++ b/solution.py
@@ -109,8 +109,8 @@
                 col_copy(0, 0 if p == 0 else 1, piece, v_hbm).start()
         row_copy(0, ON, c, v_hbm).start()
 
-    def invert(cell, carry):
-        r, c = cell // cols, cell % cols
+    def invert(r, c):
+        cell = r * cols + c
         packed = jnp.int32(0)
         for k in range(NBR):
             code = nb_ref[r, c, k]
@@ -121,9 +121,6 @@
             inv[cell * NBR + o] = entry
             total = total + entry
         inv[cell * NBR + NBR - 1] = jnp.clip(NBR * (NBR - 1) // 2 - total, 0, NBR - 1)
-        return carry
-
-    lax.fori_loop(0, rows * cols, invert, 0)
 
     v_copy.wait()
 
@@ -142,6 +139,9 @@
         kept = lax.rem(k + 1, 2)
 
         def cells(places):
+            if first:
+                for r, c in places:
+                    invert(r, c)
             for r, c in places:
                 base = (r * cols + c) * NBR
                 lhs = jnp.concatenate([hbuf[r, c, inv[base + o]] for o in range(NBR)], axis=1)
@@ -177,7 +177,7 @@
         for p in range(cols):
             j = at(p, cols)
             side = {0: 0, cols - 1: 1}.get(p)
-            if p == cols // 2 + 1:
+            if p == cols // 2:
                 hand_on(k, 1)
             if side is not None:
                 for piece in (1, 2):

time: 40 us -> 39.7 us (level)
  no operation moved by 1% of the time
where the time goes in v3:
time: 39.7 us; the launch traced here: 39.3 us
  Pallas kernels  38 us (96%)
  local copies, waits for them, and re-layouts  1.32 us (3%)
    pallas_call x1, Pallas kernels, on_device(): pl.pallas_call(functools.partial(filter_kernel, nx, ny), out_shape=jax.Sh...  38 us
    unnamed x1, local copies, waits for them, and re-layouts  1.32 us

profile of v3, /device:TPU:1, one launch (start us, length us, event | category | flops | bytes accessed | tf_op | source)
XLA Modules:
  0.0 39.3 jit_solution(2747196314475109884)
XLA Ops:
  0.0 38.0 %shard_map.37 = f32[4,8,128,128]{3,2,1,0:T(8,128)S(1)} custom-call(s32[4,8,9]{2,1,0:T(8,128)} %nb_ref.1, bf16[4,8,128,128]{3,2,1,0:T(8,128)(2,1)} %v_hbm.1, bf16[4,8,9,128,128]{4,3,2,1,0:T(8,128)(2,1)} %h_hbm.1), custom_call_target="tpu_custom_call" | custom-call | tf_op jit(solution)/shard_map/pallas_call | solution.py:227
  38.0 1.3 %copy.5 = f32[4,8,128,128]{3,2,1,0:T(8,128)} copy(f32[4,8,128,128]{3,2,1,0:T(8,128)S(1)} %shard_map.37) | data formatting | bytes 4194304

commit v4 on v3

--- a/solution.py
+++ b/solution.py
@@ -177,7 +177,7 @@
         for p in range(cols):
             j = at(p, cols)
             side = {0: 0, cols - 1: 1}.get(p)
-            if p == cols // 2:
+            if p == cols // 2 - 1:
                 hand_on(k, 1)
             if side is not None:
                 for piece in (1, 2):

time: 39.7 us -> 39.7 us (level)
  no operation moved by 1% of the time
where the time goes in v4:
time: 39.7 us; the launch traced here: 39.5 us
  Pallas kernels  38.2 us (96%)
  local copies, waits for them, and re-layouts  1.32 us (3%)
    pallas_call x1, Pallas kernels, on_device(): pl.pallas_call(functools.partial(filter_kernel, nx, ny), out_shape=jax.Sh...  38.2 us
    unnamed x1, local copies, waits for them, and re-layouts  1.32 us

profile of v4, /device:TPU:1, one launch (start us, length us, event | category | flops | bytes accessed | tf_op | source)
XLA Modules:
  0.0 39.5 jit_solution(12160016970026870321)
XLA Ops:
  0.0 38.2 %shard_map.37 = f32[4,8,128,128]{3,2,1,0:T(8,128)S(1)} custom-call(s32[4,8,9]{2,1,0:T(8,128)} %nb_ref.1, bf16[4,8,128,128]{3,2,1,0:T(8,128)(2,1)} %v_hbm.1, bf16[4,8,9,128,128]{4,3,2,1,0:T(8,128)(2,1)} %h_hbm.1), custom_call_target="tpu_custom_call" | custom-call | tf_op jit(solution)/shard_map/pallas_call | solution.py:227
  38.2 1.3 %copy.5 = f32[4,8,128,128]{3,2,1,0:T(8,128)} copy(f32[4,8,128,128]{3,2,1,0:T(8,128)S(1)} %shard_map.37) | data formatting | bytes 4194304
